TPU v7x, 32 devices: a whole 2x2x4 slice. The times are simulated.
32 devices in a mesh: wide: 8 (over z, y), narrow: 4 (over x, core).
Axes of the slice: x: 2, y: 2, z: 4, core: 2. Of those that a mesh axis runs over, the one named last changes fastest.
Arguments:
- right_side: float32 [112, 224, 256], P('narrow', 'wide'), may hold values from -60 to 60
- initial_guess: float32 [112, 224, 256], P('narrow', 'wide'), may hold values from -6 to 6
- class_map: int32 [112, 224], P('narrow', 'wide'), may hold values from 0 to 7
- class_conductivity: float32 [8], replicated, may hold values from 0.2 to 2
- window_index: int32 [4, 8, 1024], P('narrow', 'wide'), may hold values from 0 to 1023, each once within a row
- local_inverse: float32 [4, 8, 1024, 1024], P('narrow', 'wide'), may hold values from -1 to 1
- coarse_basis: float32 [4, 8, 4, 1024], P('narrow', 'wide'), may hold values from -0.1875 to 0.1875
- coarse_inverse: float32 [128, 128], P('wide', 'narrow'), may hold values from -8 to 8
Outputs:
- solution: float32 [112, 224, 256], P('narrow', 'wide')
- residual: float32 [112, 224, 256], P('narrow', 'wide')
All inputs are finite; a program needn't handle non-finite values.
Results may differ from a plain program's by a relative error of at most 0.00013.
Values sent between devices are 32-bit elements; how exact they have to be, the bound alone decides.
A program may use at most 64 MiB of HBM per device.

v0:
```python
import functools
import math

import jax
import jax.numpy as jnp
from jax import lax
from jax.experimental import pallas as pl
from jax.experimental.pallas import tpu as pltpu
from jax.sharding import PartitionSpec as P

ITERS = 3
REACTION = 0.01
LANES = 128
SUB = 8
F32 = jnp.float32
BF16 = jnp.bfloat16
MESH = pl.DeviceIdType.MESH
DIRS = ((-1, -1), (-1, 0), (-1, 1), (0, -1), (0, 1), (1, -1), (1, 0), (1, 1))

SIDES = (3, 4, 0, 2, 5, 7)
ENDS = (1, 6)


def split(value):
    high = value.astype(BF16)
    return high, (value - high.astype(F32)).astype(BF16)


def dot(left, right):
    return jnp.dot(left, right, preferred_element_type=F32)


def dot3(left_high, left_low, right_high, right_low):
    return dot(left_high, right_high) + (dot(left_low, right_high) + dot(left_high, right_low))


def kernel(
    cfg,
    rhs_ref,
    guess_ref,
    map_ref,
    class_ref,
    wrow_ref,
    inv_hbm,
    basis_ref,
    coarse_ref,
    sol_out,
    dir_out,
    res_out,
    img_out,
    size_out,
    inv_v,
    perm,
    perm_t,
    t_high,
    t_low,
    l_high,
    l_low,
    x0,
    d0,
    weights,
    phi_high,
    phi_low,
    bw,
    x_high,
    x_low,
    res,
    sol,
    img,
    deep,
    wdeep,
    z,
    kmat,
    g0,
    g,
    row0,
    col0,
    cs0,
    cor0,
    row1,
    col1,
    cs1,
    cor1,
    ssem,
    rsem,
    gs,
    gr,
    fs,
    fr,
    lsem,
    osem,
    field,
    spread,
    e_high,
    e_low,
):
    N, W, ES, OV, CS, COLS, MODES, KR = cfg
    H = OV + 1
    lo, hi = OV, OV + CS - H
    LOCAL = ES * ES
    DW = ES + 2 * SUB
    DH = ES + 2
    HALF = N // 2
    CHIPS = HALF * W
    a = lax.axis_index("narrow")
    b = lax.axis_index("wide")
    core = lax.rem(a, 2)
    me = (a // 2) * W + b

    def other(k):
        idx = lax.rem(me + k, CHIPS)
        return idx, (lax.rem(idx, W), 2 * (idx // W) + core)

    def valid(d):
        da, db = DIRS[d]
        return (a + da >= 0) & (a + da < N) & (b + db >= 0) & (b + db < W)

    barrier = pltpu.get_barrier_semaphore()

    def greet(k, carry):
        pl.semaphore_signal(barrier, inc=1, device_id=other(k)[1], device_id_type=MESH)
        return carry

    lax.fori_loop(1, CHIPS, greet, 0)
    count = CHIPS - 1
    for d, (da, db) in enumerate(DIRS):
        if da != 0:
            ok = valid(d)
            count = count + ok.astype(jnp.int32)

            @pl.when(ok)
            def _():
                pl.semaphore_signal(barrier, inc=1, device_id=(b + db, a + da), device_id_type=MESH)

    load = pltpu.make_async_copy(inv_hbm, inv_v, lsem)
    load.start()

    for d, (da, db) in enumerate(DIRS):

        @pl.when(jnp.logical_not(valid(d)))
        def _():
            for slot in range(ITERS + 1):
                if slot == 0:
                    rr, cc, kk = row0, col0, cor0
                else:
                    rr, cc, kk = row1.at[slot - 1], col1.at[slot - 1], cor1.at[slot - 1]
                if db == 0:
                    ref = rr.at[(da + 1) // 2]
                elif da == 0:
                    ref = cc.at[(db + 1) // 2]
                else:
                    ref = kk.at[(da + 1) + (db + 1) // 2]
                ref[...] = jnp.zeros(ref.shape, F32)

    step = 256
    numbering = wrow_ref[...]
    tall_numbering = jnp.transpose(jnp.broadcast_to(numbering, (LANES, LOCAL)))
    lane = lax.broadcasted_iota(jnp.int32, (LOCAL, LANES), 1)
    for c in range(0, LOCAL, LANES):
        perm_t[:, c : c + LANES] = jnp.where(lane + c == tall_numbering, 1.0, 0.0).astype(BF16)

    def hot(i, carry):
        off = pl.multiple_of(i * step, step)
        pos = lax.broadcasted_iota(jnp.int32, (step, LOCAL), 0) + off
        perm[pl.ds(off, step), :] = jnp.where(pos == numbering, 1.0, 0.0).astype(BF16)
        return carry

    lax.fori_loop(0, LOCAL // step, hot, 0)
    basis = basis_ref[0, 0]
    place = lax.rem(b, 3) * (MODES * N) + a * MODES
    line = lax.broadcasted_iota(jnp.int32, (LANES, LOCAL), 0) - place
    spread[...] = jnp.zeros(spread.shape, F32)
    for m in range(MODES):
        spread[...] = jnp.where(line == m, basis[m : m + 1], spread[...])
    b_high, b_low = split(jnp.transpose(spread[...]))
    packed = dot(perm[...], b_high) + dot(perm[...], b_low)
    x0[:, :, 2 * COLS :] = packed.reshape(ES, ES, LANES)
    classes = map_ref[...]
    conduct = jnp.zeros(classes.shape, F32)
    for k in range(class_ref.shape[0]):
        conduct = jnp.where(classes == k, class_ref[k], conduct)
    field[...] = jnp.zeros(field.shape, F32)
    field[0:CS, 0:CS] = conduct
    turned = jnp.transpose(field[...])[0:ES]
    lanes = lax.broadcasted_iota(jnp.int32, (ES, LANES), 1)
    last = lax.broadcasted_iota(jnp.int32, (CS, LANES), 1) == LANES - 1

    def fill(i, carry):
        u = OV + i
        column = jnp.sum(jnp.where(lanes == i, turned, 0.0), axis=1, keepdims=True)
        x0[u, OV : OV + CS, 0:COLS] = guess_ref[i]
        x0[u, OV : OV + CS, COLS : 2 * COLS] = rhs_ref[i]
        x0[u, OV : OV + CS, 2 * COLS :] = jnp.where(
            last, column[0:CS], x0[u, OV : OV + CS, 2 * COLS :]
        )
        return carry

    lax.fori_loop(0, CS, fill, 0)

    def strips(slot, src, rr, cc, cs, kk):
        copies = []
        for d, (da, db) in enumerate(DIRS):
            rows = pl.ds(hi if da > 0 else lo, H)
            if db == 0:
                part, dst = src.at[rows], rr.at[(1 - da) // 2]
            elif da == 0:
                part, dst = cs.at[(db + 1) // 2], cc.at[(1 - db) // 2]
            else:
                part = cs.at[(db + 1) // 2, pl.ds(0, H), pl.ds(ES - SUB if da > 0 else 0, SUB)]
                dst = kk.at[(1 - da) + (1 - db) // 2]
            copies.append(
                pltpu.make_async_remote_copy(
                    src_ref=part,
                    dst_ref=dst,
                    send_sem=ssem.at[slot, d],
                    recv_sem=rsem.at[slot, 7 - d],
                    device_id=(b + db, a + da),
                    device_id_type=MESH,
                )
            )
        return copies

    def pack(src, cs):
        def body(u, carry):
            for j in range(H):
                cs[0, j, pl.ds(u, 1), :] = src[u, lo + j : lo + j + 1, :]
                cs[1, j, pl.ds(u, 1), :] = src[u, hi + j : hi + j + 1, :]
            return carry

        lax.fori_loop(0, ES, body, 0)

    def send_strips(copies, dirs):
        for d in dirs:

            @pl.when(valid(d))
            def _():
                copies[d].start()

    def recv_strips(copies):
        for d in range(8):

            @pl.when(valid(d))
            def _():
                copies[7 - d].wait_recv()

    def done_strips(copies):
        for d in range(8):

            @pl.when(valid(d))
            def _():
                copies[d].wait_send()

    def centre(dst, src):
        def body(i, carry):
            u = OV + i
            dst[u + 1, SUB : SUB + ES, :] = src[u]
            return carry

        lax.fori_loop(0, CS, body, 0)

    def unpack(dst, rr, cc, kk):
        def sides(i, carry):
            u = OV + i
            for j in range(H):
                p = SUB - 1 + j
                dst[u + 1, p : p + 1, :] = cc[0, j, pl.ds(u, 1), :]
                p = SUB + CS + OV + j
                dst[u + 1, p : p + 1, :] = cc[1, j, pl.ds(u, 1), :]
            return carry

        lax.fori_loop(0, CS, sides, 0)
        own = slice(OV, OV + CS)
        left, right = SUB - 1, SUB + CS + OV
        base = hi - (ES - SUB)
        for side, top in ((0, 0), (1, CS + H)):
            for j in range(H):
                dst[top + j, SUB + OV : SUB + OV + CS, :] = rr[side, j, own, :]
                row = (lo if side else base) + j
                for q in range(H):
                    at = left + q
                    dst[top + j, at : at + 1, :] = kk[2 * side, q, row : row + 1, :]
                    at = right + q
                    dst[top + j, at : at + 1, :] = kk[2 * side + 1, q, row : row + 1, :]

    def coarse_copy(slot, k, ref):
        _, target = other(k)
        return pltpu.make_async_remote_copy(
            src_ref=ref.at[a, b],
            dst_ref=ref.at[a, b],
            send_sem=gs.at[slot, k],
            recv_sem=gr.at[slot, me],
            device_id=target,
            device_id_type=MESH,
        )

    def coarse_send(slot, ref):
        def body(k, carry):
            coarse_copy(slot, k, ref).start()
            return carry

        lax.fori_loop(1, CHIPS, body, 0)

    def forward(slot, i, ref):
        return pltpu.make_async_remote_copy(
            src_ref=ref.at[2 * i + core],
            dst_ref=ref.at[2 * i + core],
            send_sem=fs.at[slot, i],
            recv_sem=fr.at[slot, i],
            device_id=(b, a + 1 - 2 * core),
            device_id_type=MESH,
        )

    def coarse_relay(slot, ref):
        def body(k, carry):
            idx, target = other(k)
            pltpu.make_async_remote_copy(
                src_ref=ref.at[a, b],
                dst_ref=ref.at[target[1], target[0]],
                send_sem=gs.at[slot, k],
                recv_sem=gr.at[slot, idx],
                device_id=target,
                device_id_type=MESH,
            ).wait_recv()
            return carry

        lax.fori_loop(1, CHIPS, body, 0)
        for i in range(HALF):
            forward(slot, i, ref).start()

    def coarse_recv(slot, ref):
        for i in range(HALF):
            pltpu.make_async_remote_copy(
                src_ref=ref.at[2 * i + core],
                dst_ref=ref.at[2 * i + 1 - core],
                send_sem=fs.at[slot, i],
                recv_sem=fr.at[slot, i],
                device_id=(b, a + 1 - 2 * core),
                device_id_type=MESH,
            ).wait_recv()

    def coarse_done(slot, ref):
        def body(k, carry):
            coarse_copy(slot, k, ref).wait_send()
            return carry

        lax.fori_loop(1, CHIPS, body, 0)
        for i in range(HALF):
            forward(slot, i, ref).wait_send()

    first = strips(0, x0, row0, col0, cs0, cor0)
    pack(x0, cs0)
    pl.semaphore_wait(barrier, count)
    send_strips(first, SIDES + ENDS)
    d0[...] = jnp.zeros(d0.shape, F32)
    wdeep[...] = jnp.zeros(wdeep.shape, F32)

    load.wait()

    def right_side_perm(i, carry):
        rows = pl.ds(pl.multiple_of(i * step, step), step)
        high, low = split(inv_v[rows, :])
        t_high[rows, :] = dot(high, perm_t[...]).astype(BF16)
        t_low[rows, :] = dot(low, perm_t[...]).astype(BF16)
        return carry

    lax.fori_loop(0, LOCAL // step, right_side_perm, 0)

    def left_side_perm(i, carry):
        rows = pl.ds(pl.multiple_of(i * step, step), step)
        l_high[rows, :] = dot(perm[rows, :], t_high[...]).astype(BF16)
        l_low[rows, :] = dot(perm[rows, :], t_low[...]).astype(BF16)
        return carry

    lax.fori_loop(0, LOCAL // step, left_side_perm, 0)
    line = lax.broadcasted_iota(jnp.int32, (2 * H * ES, LOCAL), 0)
    col = line >> int(math.log2(ES))
    col = jnp.where(col < H, col + lo, col - H + hi)
    pos = (line & (ES - 1)) * ES + col
    edge = jnp.where(pos == numbering, 1.0, 0.0).astype(BF16)
    e_high[...] = dot(edge, t_high[...]).astype(BF16)
    e_low[...] = dot(edge, t_low[...]).astype(BF16)
    m_high, m_low = split(jnp.concatenate([basis, jnp.zeros((SUB - MODES, LOCAL), F32)], axis=0))
    bw[0] = dot(m_high, perm_t[...]).astype(BF16)
    bw[1] = dot(m_low, perm_t[...]).astype(BF16)

    centre(d0, x0)

    def start_sol(i, carry):
        sol[i] = x0[OV + i, :, 0:COLS]
        return carry

    lax.fori_loop(0, CS, start_sol, 0)
    recv_strips(first)
    unpack(d0, row0, col0, cor0)

    def modes(u, carry):
        value = d0[u, :, 2 * COLS :]
        high, low = split(value)
        rows = pl.ds(pl.multiple_of(u * DW, DW), DW)
        phi_high[rows, :] = high
        phi_low[rows, :] = low
        d0[u, :, 2 * COLS :] = jnp.broadcast_to(value[:, LANES - 1 : LANES], (DW, LANES))
        return carry

    lax.fori_loop(0, DH, modes, 0)
    col_pos = b * CS - OV + lax.broadcasted_iota(jnp.int32, (ES, LANES), 0)
    col_in = jnp.where((col_pos >= 0) & (col_pos < CS * W), 1.0, 0.0)

    def faces(u, carry):
        row_pos = a * CS - OV + u
        inside = jnp.where((row_pos >= 0) & (row_pos < CS * N), col_in, 0.0)
        cond = lambda du, dt: d0[u + 1 + du, SUB + dt : SUB + dt + ES, 2 * COLS :]
        own = cond(0, 0)
        half = 0.5 * inside
        weights[0, u] = REACTION * inside
        weights[1, u] = half * (own + cond(-1, 0))
        weights[2, u] = half * (own + cond(1, 0))
        weights[3, u] = half * (own + cond(0, -1))
        weights[4, u] = half * (own + cond(0, 1))
        return carry

    lax.fori_loop(0, ES, faces, 0)

    def operator(ref, u):
        parts = []
        for c in range(0, COLS, LANES):
            at = lambda du, dt: ref[u + 1 + du, SUB + dt : SUB + dt + ES, c : c + LANES]
            mid = at(0, 0)
            parts.append(
                weights[0, u] * mid
                + weights[1, u] * (mid - at(-1, 0))
                + weights[2, u] * (mid - at(1, 0))
                + weights[3, u] * (mid - at(0, -1))
                + weights[4, u] * (mid - at(0, 1))
            )
        return jnp.concatenate(parts, axis=1)

    def set_x(u, value):
        high, low = split(value)
        rows = pl.ds(pl.multiple_of(u * ES, ES), ES)
        x_high[rows, :] = high
        x_low[rows, :] = low

    def first_residual(u, carry):
        inside = jnp.where(weights[0, u] > 0.0, 1.0, 0.0)
        inside = jnp.concatenate([inside] * (COLS // LANES), axis=1)
        right = d0[u + 1, SUB : SUB + ES, COLS : 2 * COLS]
        value = right * inside - operator(d0, u)
        res[u] = value
        set_x(u, value)
        return carry

    lax.fori_loop(0, ES, first_residual, 0)

    def coarse_rows():
        return dot3(bw[0], bw[1], x_high[...], x_low[...])

    sub_pos = lax.broadcasted_iota(jnp.int32, (SUB, COLS), 0)
    pending = []
    numer = denom = None
    for it in range(ITERS + 1):
        ref = g0 if it == 0 else g.at[it - 1]
        if it == 0:
            ref[a, b] = jnp.zeros((ref.shape[2], COLS), F32)
            ref[a, b, 0:SUB, :] = coarse_rows()
            run = MODES * W
            for i in range(MODES * N):
                line, at = divmod(i * run, COLS)
                ref[a, b, MODES + line, at : at + run] = coarse_ref[i]
        else:
            rows = coarse_rows() if it < ITERS else jnp.zeros((SUB, COLS), F32)
            rows = jnp.where(sub_pos == MODES, numer, rows)
            rows = jnp.where(sub_pos == MODES + 1, denom, rows)
            ref[a, b] = rows
        coarse_send(it, ref)
        if it == ITERS:
            own = pl.ds(OV, CS)
            pairs = (
                (sol, sol_out),
                (deep.at[pl.ds(OV + 1, CS), pl.ds(SUB, ES)], dir_out),
                (res.at[own], res_out),
                (img.at[own], img_out),
            )
            writes = [
                pltpu.make_async_copy(src, dst, osem.at[n]) for n, (src, dst) in enumerate(pairs)
            ]
            for copy in writes:
                copy.start()
        if it < ITERS:
            value = dot3(e_high[...], e_low[...], x_high[...], x_low[...])
            cs1[it] = value.reshape(2, H, ES, COLS)
            copies = strips(it + 1, z.at[it], row1.at[it], col1.at[it], cs1.at[it], cor1.at[it])
            send_strips(copies, SIDES)

            def solve(i, carry):
                rows = pl.ds(pl.multiple_of(i * step, step), step)
                value = dot3(l_high[rows, :], l_low[rows, :], x_high[...], x_low[...])
                z[it, pl.ds(i * (step // ES), step // ES)] = value.reshape(step // ES, ES, COLS)
                return carry

            lax.fori_loop(0, LOCAL // step, solve, 0)
            send_strips(copies, ENDS)
            centre(wdeep, z.at[it])
            pending.append(copies)
        coarse_relay(it, ref)
        coarse_recv(it, ref)
        if it == 0:
            per = COLS // (4 * W)
            wide_cols = MODES * W
            group = MODES * N
            piece = lax.broadcasted_iota(jnp.int32, (group, COLS), 0) & (per - 1)
            lane = lax.broadcasted_iota(jnp.int32, (group, COLS), 1)
            keep = (lane >> int(math.log2(wide_cols))) == piece
            width = N * W * SUB
            j = lax.broadcasted_iota(jnp.int32, (COLS, width), 0) & (wide_cols - 1)
            c = lax.broadcasted_iota(jnp.int32, (COLS, width), 1)
            total_high = total_low = None
            for a2 in range(N):
                blocks = []
                for third in range(3):
                    db = lax.rem(third - b + 1 + 3 * W, 3) - 1
                    at = jnp.clip(b + db, 0, W - 1)
                    raw = ref[a2, at, MODES : MODES + KR, :]
                    tall = jnp.concatenate(
                        [jnp.broadcast_to(raw[r : r + 1], (per, COLS)) for r in range(KR)], axis=0
                    )
                    blocks.append(jnp.where(keep, tall, 0.0))
                blocks.append(jnp.zeros((LANES - 3 * group, COLS), F32))
                high, low = split(jnp.concatenate(blocks, axis=0))
                fold = c == a2 * (W * SUB) + (j >> 2) * SUB + (j & 3)
                fold = jnp.where(fold, 1.0, 0.0).astype(BF16)
                th, tl = dot(high, fold), dot(low, fold)
                total_high = th if total_high is None else total_high + th
                total_low = tl if total_low is None else total_low + tl
            kmat[0] = total_high.astype(BF16)
            kmat[1] = total_low.astype(BF16)
        else:
            total = jnp.sum(ref[...].reshape(N * W, SUB, COLS), axis=0)
            size = total[MODES : MODES + 1] / total[MODES + 1 : MODES + 2]
        if it == ITERS:
            break
        g_high, g_low = split(ref[:, :, 0:SUB, :].reshape(N * W * SUB, COLS))
        s_high, s_low = split(dot3(kmat[0], kmat[1], g_high, g_low))
        if it > 0:

            def advance(i, carry):
                u = OV + i
                sol[i] = sol[i] + size * deep[u + 1, SUB : SUB + ES, :]
                res[u] = res[u] - size * img[u]
                return carry

            lax.fori_loop(0, CS, advance, 0)
        recv_strips(copies)
        unpack(wdeep, row1.at[it], col1.at[it], cor1.at[it])
        chunk = DH // 2

        def coarse_part(i, carry):
            rows = pl.ds(pl.multiple_of(i * chunk * DW, chunk * DW), chunk * DW)
            value = dot3(phi_high[rows, :], phi_low[rows, :], s_high, s_low)
            tall = pl.ds(i * chunk, chunk)
            value = value.reshape(chunk, DW, COLS) + wdeep[tall]
            if it == 0:
                deep[tall] = value
            else:
                deep[tall] = deep[tall] - size * value
            return carry

        lax.fori_loop(0, 2, coarse_part, 0)

        def apply(u, carry):
            top, bottom = carry
            value = operator(deep, u)
            img[u] = value
            if it < ITERS - 1:
                set_x(u, value)
            own = jnp.where((u >= OV) & (u < OV + CS), value, 0.0)
            return top + res[u] * own, bottom + value * own

        nothing = jnp.zeros((ES, COLS), F32)
        top, bottom = lax.fori_loop(0, ES, apply, (nothing, nothing))
        col = lax.broadcasted_iota(jnp.int32, (ES, COLS), 0)
        mine = (col >= OV) & (col < OV + CS)
        numer = jnp.sum(jnp.where(mine, top, 0.0), axis=0, keepdims=True)
        denom = jnp.sum(jnp.where(mine, bottom, 0.0), axis=0, keepdims=True)

    done_strips(first)
    for copies in pending:
        done_strips(copies)
    size_out[...] = jnp.broadcast_to(size, (SUB, COLS))
    for copy in writes:
        copy.wait()
    for it in range(ITERS + 1):
        coarse_done(it, g0 if it == 0 else g.at[it - 1])


def finish(OV, CS, sol, direction, res, image, size, sol_out, res_out):
    step = size[0:1]
    for i in range(sol.shape[0]):
        sol_out[i] = (sol[i] + step * direction[i])[OV : OV + CS]
        res_out[i] = (res[i] - step * image[i])[OV : OV + CS]


def local(
    N,
    W,
    right_side,
    initial_guess,
    class_map,
    class_conductivity,
    window_index,
    local_inverse,
    coarse_basis,
    coarse_inverse,
):
    CS, _, COLS = right_side.shape
    MODES, LOCAL = coarse_basis.shape[2:]
    ES = math.isqrt(LOCAL)
    OV = (ES - CS) // 2
    H = OV + 1
    DW, DH = ES + 2 * SUB, ES + 2
    KR = coarse_inverse.size // COLS
    R0 = -(-(MODES + KR) // SUB) * SUB
    CHIPS = N * W // 2
    vmem = pl.BlockSpec(memory_space=pltpu.VMEM)
    big = 2 * COLS + LANES
    scratch = [
        pltpu.VMEM((LOCAL, LOCAL), F32),
        pltpu.VMEM((LOCAL, LOCAL), BF16),
        pltpu.VMEM((LOCAL, LOCAL), BF16),
        pltpu.VMEM((LOCAL, LOCAL), BF16),
        pltpu.VMEM((LOCAL, LOCAL), BF16),
        pltpu.VMEM((LOCAL, LOCAL), BF16),
        pltpu.VMEM((LOCAL, LOCAL), BF16),
        pltpu.VMEM((ES, ES, big), F32),
        pltpu.VMEM((DH, DW, big), F32),
        pltpu.VMEM((5, ES, ES, LANES), F32),
        pltpu.VMEM((DH * DW, LANES), BF16),
        pltpu.VMEM((DH * DW, LANES), BF16),
        pltpu.VMEM((2, SUB, LOCAL), BF16),
        pltpu.VMEM((LOCAL, COLS), BF16),
        pltpu.VMEM((LOCAL, COLS), BF16),
        pltpu.VMEM((ES, ES, COLS), F32),
        pltpu.VMEM((CS, ES, COLS), F32),
        pltpu.VMEM((ES, ES, COLS), F32),
        pltpu.VMEM((DH, DW, COLS), F32),
        pltpu.VMEM((DH, DW, COLS), F32),
        pltpu.VMEM((ITERS, ES, ES, COLS), F32),
        pltpu.VMEM((2, LANES, N * W * SUB), BF16),
        pltpu.VMEM((N, W, R0, COLS), F32),
        pltpu.VMEM((ITERS, N, W, SUB, COLS), F32),
        pltpu.VMEM((2, H, ES, big), F32),
        pltpu.VMEM((2, H, ES, big), F32),
        pltpu.VMEM((2, H, ES, big), F32),
        pltpu.VMEM((4, H, SUB, big), F32),
        pltpu.VMEM((ITERS, 2, H, ES, COLS), F32),
        pltpu.VMEM((ITERS, 2, H, ES, COLS), F32),
        pltpu.VMEM((ITERS, 2, H, ES, COLS), F32),
        pltpu.VMEM((ITERS, 4, H, SUB, COLS), F32),
        pltpu.SemaphoreType.DMA((ITERS + 1, 8)),
        pltpu.SemaphoreType.DMA((ITERS + 1, 8)),
        pltpu.SemaphoreType.DMA((ITERS + 1, CHIPS)),
        pltpu.SemaphoreType.DMA((ITERS + 1, CHIPS)),
        pltpu.SemaphoreType.DMA((ITERS + 1, N // 2)),
        pltpu.SemaphoreType.DMA((ITERS + 1, N // 2)),
        pltpu.SemaphoreType.DMA,
        pltpu.SemaphoreType.DMA((4,)),
        pltpu.VMEM((LANES, LANES), F32),
        pltpu.VMEM((LANES, LOCAL), F32),
        pltpu.VMEM((2 * H * ES, LOCAL), BF16),
        pltpu.VMEM((2 * H * ES, LOCAL), BF16),
    ]
    out = jax.ShapeDtypeStruct((CS, ES, COLS), F32)
    anywhere = pl.BlockSpec(memory_space=pl.ANY)
    smem = pl.BlockSpec(memory_space=pltpu.SMEM)
    *fields, size = pl.pallas_call(
        functools.partial(kernel, (N, W, ES, OV, CS, COLS, MODES, KR)),
        out_shape=(out,) * 4 + (jax.ShapeDtypeStruct((SUB, COLS), F32),),
        in_specs=[vmem] * 3 + [smem, vmem, anywhere] + [vmem] * 2,
        out_specs=(anywhere,) * 4 + (vmem,),
        scratch_shapes=scratch,
        compiler_params=pltpu.CompilerParams(
            collective_id=0, has_side_effects=True, vmem_limit_bytes=67043328
        ),
        name="schwarz",
    )(
        right_side,
        initial_guess,
        class_map,
        class_conductivity,
        window_index[0],
        local_inverse[0, 0],
        coarse_basis,
        coarse_inverse,
    )
    block = CS // 4
    part = pl.BlockSpec((block, ES, COLS), lambda i: (i, 0, 0))
    done = pl.BlockSpec((block, CS, COLS), lambda i: (i, 0, 0))
    return pl.pallas_call(
        functools.partial(finish, OV, CS),
        grid=(CS // block,),
        out_shape=(jax.ShapeDtypeStruct(right_side.shape, F32),) * 2,
        in_specs=[part] * 4 + [pl.BlockSpec((SUB, COLS), lambda i: (0, 0))],
        out_specs=(done, done),
        name="finish",
    )(*fields, size)


def solution(mesh):
    in_specs = (
        P("narrow", "wide", None),
        P("narrow", "wide", None),
        P("narrow", "wide"),
        P(),
        P("narrow", "wide", None),
        P("narrow", "wide", None, None),
        P("narrow", "wide", None, None),
        P("wide", "narrow"),
    )
    out_specs = (P("narrow", "wide", None), P("narrow", "wide", None))
    body = functools.partial(local, mesh.shape["narrow"], mesh.shape["wide"])
    return jax.shard_map(body, mesh=mesh, in_specs=in_specs, out_specs=out_specs, check_vma=False)
```

profile of v0, /device:TPU:1, one launch (start us, length us, event | category | flops | bytes accessed | tf_op | source)
XLA Modules:
  0.0 79.5 jit_solution(15336388003700147197)
XLA Ops:
  0.6 74.7 %schwarz.1 = (f32[28,32,256]{2,1,0:T(8,128)}, f32[28,32,256]{2,1,0:T(8,128)}, f32[28,32,256]{2,1,0:T(8,128)}, f32[28,32,256]{2,1,0:T(8,128)}, f32[8,256]{1,0:T(8,128)}) custom-call(f32[28,28,256]{2,1,0:T(8,128)} %rhs_ref.1, f32[28,28,256]{2,1,0:T(8,128)} %guess_ref.1, s32[28,28]{1,0:T(8,128)} %map_ref.1, f32[8]{0:T(128)} %class_ref.1, s32[1,1024]{1,0:T(1,128)} %bitcast.3, ...), custom_call_target="tpu_custom_call" | custom-call | tf_op jit(solution)/shard_map/schwarz/pallas_call | solution.py:675
  75.3 4.2 %finish.1 = (f32[28,28,256]{2,1,0:T(8,128)}, f32[28,28,256]{2,1,0:T(8,128)}) custom-call(f32[28,32,256]{2,1,0:T(8,128)} %get-tuple-element.7.sol, f32[28,32,256]{2,1,0:T(8,128)} %get-tuple-element.8.direction, f32[28,32,256]{2,1,0:T(8,128)} %get-tuple-element.9.res, f32[28,32,256]{2,1,0:T(8,128)} %get-tuple-element.10.image, f32[8,256]{1,0:T(8,128)} %get-tuple-element.11.size), custom_call_target="tpu_custom_call" | custom-call | tf_op jit(solution)/shard_map/finish/pallas_call | solution.py:698
where the time goes:
time: 79.7 us; the launch traced here: 79.5 us
  Pallas kernels  78.8 us (99%)
    pallas_call x1, Pallas kernels, local(): pl.pallas_call(functools.partial(kernel, (N, W, ES, OV, CS, COLS, MODES,...  74.7 us
    pallas_call x1, Pallas kernels, local(): pl.pallas_call(functools.partial(finish, OV, CS), grid=(CS // block,), ou...  4.15 us

commit v1 on v0

v1 whole, which is shorter than its diff:
```python
import functools
import math
import types

import jax
import jax.numpy as jnp
from jax import lax
from jax.experimental import pallas as pl
from jax.experimental.pallas import tpu as pltpu
from jax.sharding import PartitionSpec as P

ITERS = 3
REACTION = 0.01
LANES = 128
SUB = 8
F32 = jnp.float32
BF16 = jnp.bfloat16
MESH = pl.DeviceIdType.MESH
DIRS = ((-1, -1), (-1, 0), (-1, 1), (0, -1), (0, 1), (1, -1), (1, 0), (1, 1))

SIDES = (3, 4, 0, 2, 5, 7)
ENDS = (1, 6)


def split(value):
    high = value.astype(BF16)
    return high, (value - high.astype(F32)).astype(BF16)


def dot(left, right):
    return jnp.dot(left, right, preferred_element_type=F32)


def dot3(left_high, left_low, right_high, right_low):
    return dot(left_high, right_high) + (dot(left_low, right_high) + dot(left_high, right_low))


def half(h):
    return slice(h * LANES, (h + 1) * LANES)


def kernel(cfg, names, *refs):
    N, W, ES, OV, CS, COLS, MODES, KR = cfg
    rhs_ref, guess_ref, map_ref, class_ref, wrow_ref, inv_hbm, basis_ref, coarse_ref = refs[:8]
    sol_out, res_out = refs[8:10]
    s = types.SimpleNamespace(**dict(zip(names, refs[10:])))
    H = OV + 1
    lo, hi = OV, OV + CS - H
    LOCAL = ES * ES
    DW = ES + 2
    RP = s.daux.shape[0]
    HV = COLS // LANES
    LK = 3 * MODES * N
    HALF = N // 2
    CHIPS = HALF * W
    base = hi - (ES - SUB)
    a = lax.axis_index("narrow")
    b = lax.axis_index("wide")
    core = lax.rem(a, 2)
    me = (a // 2) * W + b

    def at(u, t):
        return (u + 1) * DW + t + 1

    def other(k):
        idx = lax.rem(me + k, CHIPS)
        return idx, (lax.rem(idx, W), 2 * (idx // W) + core)

    def valid(d):
        da, db = DIRS[d]
        return (a + da >= 0) & (a + da < N) & (b + db >= 0) & (b + db < W)

    barrier = pltpu.get_barrier_semaphore()

    def greet(k, carry):
        pl.semaphore_signal(barrier, inc=1, device_id=other(k)[1], device_id_type=MESH)
        return carry

    lax.fori_loop(1, CHIPS, greet, 0)
    count = CHIPS - 1
    for d, (da, db) in enumerate(DIRS):
        if da != 0:
            ok = valid(d)
            count = count + ok.astype(jnp.int32)

            @pl.when(ok)
            def _():
                pl.semaphore_signal(barrier, inc=1, device_id=(b + db, a + da), device_id_type=MESH)

    load = pltpu.make_async_copy(inv_hbm, s.inv, s.lsem)
    load.start()

    def landing(d, rows, cols, corners, away):
        da, db = DIRS[d]
        if away:
            da, db = -da, -db
        if db == 0:
            return rows((da + 1) // 2)
        if da == 0:
            return cols((db + 1) // 2)
        return corners((da + 1) + (db + 1) // 2)

    groups = [
        (s.g_row, s.g_col, None),
        (s.c_row, s.c_col, s.c_cor),
        (s.a_row, s.a_col, s.a_cor),
        (s.r_row, s.r_col, s.r_cor),
    ]
    groups += [(s.z_row.at[i], s.z_col.at[i], s.z_cor.at[i]) for i in range(ITERS)]

    for d in range(8):

        @pl.when(jnp.logical_not(valid(d)))
        def _():
            for rows, cols, corners in groups:
                if corners is None and 0 not in DIRS[d]:
                    continue
                pick = lambda ref: lambda i: ref.at[i]
                ref = landing(d, pick(rows), pick(cols), corners is not None and pick(corners), False)
                ref[...] = jnp.zeros(ref.shape, F32)

    def exchange(slot, rows, cols, corners):
        copies = {}
        for d in range(8):
            if corners is None and 0 not in DIRS[d]:
                continue
            da, db = DIRS[d]
            to = groups[slot]
            pick = lambda ref: lambda i: ref.at[i]
            copies[d] = pltpu.make_async_remote_copy(
                src_ref=landing(d, rows, cols, corners, False),
                dst_ref=landing(d, pick(to[0]), pick(to[1]), to[2] is not None and pick(to[2]), True),
                send_sem=s.ssem.at[slot, d],
                recv_sem=s.rsem.at[slot, 7 - d],
                device_id=(b + db, a + da),
                device_id_type=MESH,
            )
        return copies

    def send(copies, dirs=SIDES + ENDS):
        for d in dirs:
            if d in copies:

                @pl.when(valid(d))
                def _():
                    copies[d].start()

    def recv(copies):
        for d in copies:

            @pl.when(valid(d))
            def _():
                copies[7 - d].wait_recv()

    def done(copies):
        for d in copies:

            @pl.when(valid(d))
            def _():
                copies[d].wait_send()

    def gather_copy(slot, k, ref, rows):
        _, target = other(k)
        part = ref.at[a, b, rows]
        return pltpu.make_async_remote_copy(
            src_ref=part,
            dst_ref=part,
            send_sem=s.gs.at[slot, k],
            recv_sem=s.gr.at[slot, me],
            device_id=target,
            device_id_type=MESH,
        )

    def forward(slot, k, ref, rows, mine):
        idx, _ = other(k)
        row = 2 * (idx // W)
        part = ref.at[row + core, lax.rem(idx, W), rows]
        away = part if mine else ref.at[row + 1 - core, lax.rem(idx, W), rows]
        return pltpu.make_async_remote_copy(
            src_ref=part,
            dst_ref=away,
            send_sem=s.fs.at[slot, k],
            recv_sem=s.fr.at[slot, idx],
            device_id=(b, a + 1 - 2 * core),
            device_id_type=MESH,
        )

    def gather_send(slot, ref, rows):
        def body(k, carry):
            gather_copy(slot, k, ref, rows).start()
            return carry

        lax.fori_loop(1, CHIPS, body, 0)
        forward(slot, 0, ref, rows, True).start()

    def gather_recv(slot, ref, rows):
        def relay(k, carry):
            idx, target = other(k)
            pltpu.make_async_remote_copy(
                src_ref=ref.at[a, b, rows],
                dst_ref=ref.at[target[1], target[0], rows],
                send_sem=s.gs.at[slot, k],
                recv_sem=s.gr.at[slot, idx],
                device_id=target,
                device_id_type=MESH,
            ).wait_recv()
            forward(slot, k, ref, rows, True).start()
            return carry

        lax.fori_loop(1, CHIPS, relay, 0)

        def collect(k, carry):
            forward(slot, k, ref, rows, False).wait_recv()
            return carry

        lax.fori_loop(0, CHIPS, collect, 0)

    def gather_done(slot, ref, rows):
        def body(k, carry):
            gather_copy(slot, k, ref, rows).wait_send()
            return carry

        lax.fori_loop(1, CHIPS, body, 0)

        def sent(k, carry):
            forward(slot, k, ref, rows, True).wait_send()
            return carry

        lax.fori_loop(0, CHIPS, sent, 0)

    def edges_of_guess(i, carry):
        s.gs_col[0, pl.ds(i, 1), :] = guess_ref[i, 0:1, :]
        s.gs_col[1, pl.ds(i, 1), :] = guess_ref[i, CS - 1 : CS, :]
        return carry

    lax.fori_loop(0, CS, edges_of_guess, 0)
    classes = map_ref[...]
    conduct = jnp.zeros(classes.shape, F32)
    for k in range(class_ref.shape[0]):
        conduct = jnp.where(classes == k, class_ref[k], conduct)
    s.field[...] = jnp.zeros(s.field.shape, F32)
    s.field[0:CS, 0:CS] = conduct
    s.cfield[...] = jnp.transpose(s.field[...])[0:ES]
    run = MODES * W
    for i in range(MODES * N):
        line, left = divmod(i * run, COLS)
        s.k0[a, b, line : line + 1, left : left + run] = coarse_ref[i : i + 1]

    guess_sends = exchange(
        0, lambda i: guess_ref.at[i * (CS - 1)], lambda i: s.gs_col.at[i], None
    )
    tile = lambda i: s.cfield.at[pl.ds(i * (ES - SUB), SUB)]
    cond_sends = exchange(1, lambda i: s.cfield, tile, lambda i: tile(i % 2))
    pl.semaphore_wait(barrier, count)
    send(cond_sends)
    send(guess_sends)
    k_rows = pl.ds(0, KR)
    gather_send(0, s.k0, k_rows)

    step = 256
    numbering = wrow_ref[...]
    tall_numbering = jnp.transpose(jnp.broadcast_to(numbering, (LANES, LOCAL)))
    lane = lax.broadcasted_iota(jnp.int32, (LOCAL, LANES), 1)
    for c in range(0, LOCAL, LANES):
        s.perm_t[:, c : c + LANES] = jnp.where(lane + c == tall_numbering, 1.0, 0.0).astype(BF16)

    def hot(i, carry):
        off = pl.multiple_of(i * step, step)
        pos = lax.broadcasted_iota(jnp.int32, (step, LOCAL), 0) + off
        s.perm[pl.ds(off, step), :] = jnp.where(pos == numbering, 1.0, 0.0).astype(BF16)
        return carry

    lax.fori_loop(0, LOCAL // step, hot, 0)
    basis = basis_ref[0, 0]
    place = lax.rem(b, 3) * (MODES * N) + a * MODES
    line = lax.broadcasted_iota(jnp.int32, (LANES, LOCAL), 0) - place
    s.spread[...] = jnp.zeros(s.spread.shape, F32)
    for m in range(MODES):
        s.spread[...] = jnp.where(line == m, basis[m : m + 1], s.spread[...])
    b_high, b_low = split(jnp.transpose(s.spread[...]))
    s.aux[...] = dot(s.perm[...], b_high) + dot(s.perm[...], b_low)
    for k, first in enumerate((lo, hi)):
        for j in range(H):
            s.as_col[k, j] = s.aux[pl.ds(first + j, ES, stride=ES), :]
    aux_sends = exchange(
        2,
        lambda i: s.aux.at[pl.ds((lo, hi)[i] * ES, H * ES)],
        lambda i: s.as_col.at[i],
        lambda i: s.as_col.at[i % 2, pl.ds(0, H), pl.ds((ES - SUB) * (i // 2), SUB)],
    )

    def place_guess(i, carry):
        for h in range(HV):
            s.gd[h, pl.ds(at(OV + i, OV), CS), :] = guess_ref[i, :, half(h)]
            s.sol[h, i, 0:CS, :] = guess_ref[i, :, half(h)]
        return carry

    lax.fori_loop(0, CS, place_guess, 0)
    recv(guess_sends)
    recv(cond_sends)
    for h in range(HV):
        for side in range(2):
            edge = OV - 1 + side * (CS + 1)
            s.gd[h, pl.ds(at(edge, OV), CS), :] = s.g_row[side, :, half(h)]
            s.gd[h, pl.ds(at(OV, edge), CS, stride=DW), :] = s.g_col[side, :, half(h)]
    stack = (
        (s.c_cor.at[0], s.c_row.at[0], s.c_cor.at[1]),
        (s.c_col.at[0], s.cfield, s.c_col.at[1]),
        (s.c_cor.at[2], s.c_row.at[1], s.c_cor.at[3]),
    )
    for k, (left, mid, right) in enumerate(stack):
        s.cst[k, 0:H] = left[CS - H - (ES - SUB) : CS - (ES - SUB)]
        s.cst[k, H : H + CS] = mid[0:CS]
        s.cst[k, H + CS : DW] = right[0:H]
    clane = lax.broadcasted_iota(jnp.int32, s.cst.shape[1:], 1)
    cmap = jnp.where(
        clane < H,
        pltpu.roll(s.cst[0], LANES - (CS - H), 1),
        jnp.where(
            clane < H + CS, pltpu.roll(s.cst[1], H, 1), pltpu.roll(s.cst[2], H + CS, 1)
        ),
    )
    for r in range(DW):
        s.cond[pl.ds(r * DW, DW), :] = jnp.broadcast_to(cmap[0:DW, r : r + 1], (DW, LANES))
    col_pos = b * CS - OV + lax.broadcasted_iota(jnp.int32, (ES, LANES), 0)
    col_in = jnp.where((col_pos >= 0) & (col_pos < CS * W), 1.0, 0.0)

    def faces(u, carry):
        row_pos = a * CS - OV + u
        inside = jnp.where((row_pos >= 0) & (row_pos < CS * N), col_in, 0.0)
        cond = lambda du, dt: s.cond[pl.ds(at(u + du, dt), ES), :]
        own = cond(0, 0)
        halved = 0.5 * inside
        parts = [halved * (own + cond(*o)) for o in ((-1, 0), (1, 0), (0, -1), (0, 1))]
        here = pl.ds(pl.multiple_of(u * ES, ES), ES)
        s.wt[0, here, :] = REACTION * inside + ((parts[0] + parts[1]) + (parts[2] + parts[3]))
        for k in range(4):
            s.wt[1 + k, here, :] = parts[k]
        return carry

    lax.fori_loop(0, ES, faces, 0)

    def operator(read, u, t, n):
        weights = [s.wt[k, pl.ds(u * ES + t, n), :] for k in range(5)]
        out = []
        for h in range(HV):
            v = lambda du, dt: read(h, pl.ds(at(u + du, t + dt), n))
            around = weights[1] * v(-1, 0) + weights[2] * v(1, 0)
            beside = weights[3] * v(0, -1) + weights[4] * v(0, 1)
            out.append(weights[0] * v(0, 0) - (around + beside))
        return out

    def own_residual(i, carry):
        u = OV + i
        image = operator(lambda h, rows: s.gd[h, rows, :], u, OV, CS)
        for h in range(HV):
            s.res[h, pl.ds(u * ES + OV, CS), :] = rhs_ref[i, :, half(h)] - image[h]
        return carry

    lax.fori_loop(0, CS, own_residual, 0)

    near = (OV, CS)
    for k in range(2):
        for h in range(HV):
            for q in range(OV):
                s.rs_col[k, h, q] = s.res[h, pl.ds(near[k] + q, ES, stride=ES), :]
            s.rs_row[k, h] = s.res[h, near[k] * ES : (near[k] + OV) * ES, :]
    for k in range(4):
        for h in range(HV):
            for r in range(OV):
                cell = (near[k // 2] + r) * ES + near[k % 2]
                s.rs_cor[k, h, r * OV : (r + 1) * OV, :] = s.res[h, cell : cell + OV, :]
    res_sends = exchange(
        3,
        lambda i: s.rs_row.at[i],
        lambda i: s.rs_col.at[i],
        lambda i: s.rs_cor.at[i],
    )
    send(res_sends)
    send(aux_sends)

    load.wait()

    def right_side_perm(i, carry):
        rows = pl.ds(pl.multiple_of(i * step, step), step)
        high, low = split(s.inv[rows, :])
        s.t_high[rows, :] = dot(high, s.perm_t[...]).astype(BF16)
        s.t_low[rows, :] = dot(low, s.perm_t[...]).astype(BF16)
        return carry

    lax.fori_loop(0, LOCAL // step, right_side_perm, 0)
    line = lax.broadcasted_iota(jnp.int32, (2 * H * ES, LOCAL), 0)
    col = line >> int(math.log2(ES))
    col = jnp.where(col < H, col + lo, col - H + hi)
    pos = (line & (ES - 1)) * ES + col
    edge = jnp.where(pos == numbering, 1.0, 0.0).astype(BF16)
    s.e_high[...] = dot(edge, s.t_high[...]).astype(BF16)
    s.e_low[...] = dot(edge, s.t_low[...]).astype(BF16)
    m_high, m_low = split(jnp.concatenate([basis, jnp.zeros((SUB - MODES, LOCAL), F32)], axis=0))
    s.bw[...] = dot(jnp.concatenate([m_high, m_low], axis=0), s.perm_t[...]).astype(BF16)

    def set_x(u, value):
        high, low = split(jnp.concatenate(value, axis=1))
        rows = pl.ds(pl.multiple_of(u * ES, ES), ES)
        s.x_high[rows, :] = high
        s.x_low[rows, :] = low

    recv(res_sends)
    far = (0, OV + CS)
    for h in range(HV):
        for k in range(2):
            for q in range(OV):
                line = slice(q * ES + OV, q * ES + OV + CS)
                s.res[h, pl.ds((far[k] + q) * ES + OV, CS), :] = s.r_row[k, h, line, :]
                line = pl.ds(OV * ES + far[k] + q, CS, stride=ES)
                s.res[h, line, :] = s.r_col[k, h, q, OV : OV + CS, :]
        for k in range(4):
            for r in range(OV):
                cell = (far[k // 2] + r) * ES + far[k % 2]
                s.res[h, cell : cell + OV, :] = s.r_cor[k, h, r * OV : (r + 1) * OV, :]

    def first_x(u, carry):
        set_x(u, [s.res[h, pl.ds(u * ES, ES), :] for h in range(HV)])
        return carry

    lax.fori_loop(0, ES, first_x, 0)

    def coarse_rows():
        both = dot(s.bw[...], s.x_high[...])
        return both[0:SUB] + (both[SUB:] + dot(s.bw[0:SUB, :], s.x_low[...]))

    def left_side_perm(i, carry):
        rows = pl.ds(pl.multiple_of(i * step, step), step)
        s.l_high[rows, :] = dot(s.perm[rows, :], s.t_high[...]).astype(BF16)
        s.l_low[rows, :] = dot(s.perm[rows, :], s.t_low[...]).astype(BF16)
        return carry

    def build_phi():
        recv(aux_sends)
        for i in range(CS):
            s.daux[pl.ds(at(OV + i, OV), CS), :] = s.aux[pl.ds((OV + i) * ES + OV, CS), :]
        for k in range(2):
            for j in range(H):
                deep_line = k * (CS + H) + j
                s.daux[pl.ds(deep_line * DW + H, CS), :] = s.a_row[
                    k, j * ES + OV : j * ES + OV + CS, :
                ]
                s.daux[pl.ds(H * DW + deep_line, CS, stride=DW), :] = s.a_col[
                    k, j, OV : OV + CS, :
                ]
        for k in range(4):
            first = lo if k // 2 else base
            for q in range(H):
                cell = (k // 2) * (CS + H) * DW + (k % 2) * (CS + H) + q
                for r in range(H):
                    s.daux[pl.ds(cell + r * DW, 1), :] = s.a_cor[k, q, first + r : first + r + 1, :]
        chunk = RP // 2

        def body(i, carry):
            rows = pl.ds(pl.multiple_of(i * chunk, chunk), chunk)
            value = s.daux[rows, :]
            high = value.astype(BF16).astype(F32)
            low = value - high
            if 2 * LK <= LANES:
                s.phi[rows, 0:LANES] = (high + pltpu.roll(low, LK, 1)).astype(BF16)
                s.phi[rows, LANES:] = high.astype(BF16)
            else:
                s.phi[rows, 0:LANES] = high.astype(BF16)
                s.phi[rows, LANES : 2 * LANES] = low.astype(BF16)
                s.phi[rows, 2 * LANES :] = high.astype(BF16)
            return carry

        lax.fori_loop(0, 2, body, 0)

    def build_kmat():
        gather_recv(0, s.k0, k_rows)
        per = COLS // (4 * W)
        wide_cols = MODES * W
        group = MODES * N
        piece = lax.broadcasted_iota(jnp.int32, (group, COLS), 0) & (per - 1)
        lane = lax.broadcasted_iota(jnp.int32, (group, COLS), 1)
        keep = (lane >> int(math.log2(wide_cols))) == piece
        width = N * W * SUB
        j = lax.broadcasted_iota(jnp.int32, (COLS, width), 0) & (wide_cols - 1)
        c = lax.broadcasted_iota(jnp.int32, (COLS, width), 1)
        total_high = total_low = None
        for a2 in range(N):
            blocks = []
            for third in range(3):
                db = lax.rem(third - b + 1 + 3 * W, 3) - 1
                spot = jnp.clip(b + db, 0, W - 1)
                raw = s.k0[a2, spot, 0:KR, :]
                tall = jnp.concatenate(
                    [jnp.broadcast_to(raw[r : r + 1], (per, COLS)) for r in range(KR)], axis=0
                )
                blocks.append(jnp.where(keep, tall, 0.0))
            if 2 * LK <= LANES:
                blocks = blocks * 2
            fill = LANES - len(blocks) * group
            blocks.append(jnp.zeros((fill, COLS), F32))
            high, low = split(jnp.concatenate(blocks, axis=0))
            fold = c == a2 * (W * SUB) + (j >> 2) * SUB + (j & 3)
            fold = jnp.where(fold, 1.0, 0.0).astype(BF16)
            th, tl = dot(high, fold), dot(low, fold)
            total_high = th if total_high is None else total_high + th
            total_low = tl if total_low is None else total_low + tl
        s.kmat[0] = total_high.astype(BF16)
        s.kmat[1] = total_low.astype(BF16)

    sub_pos = lax.broadcasted_iota(jnp.int32, (SUB, COLS), 0)
    pending = [guess_sends, cond_sends, aux_sends, res_sends]
    numer = denom = None
    sizes = []
    spans = []
    for it in range(ITERS + 1):
        ref = s.g.at[it]
        first = MODES if it == ITERS else 0
        last = MODES if it == 0 else MODES + 2
        span = pl.ds(first, last - first)
        spans.append(span)
        rows = coarse_rows() if it < ITERS else jnp.zeros((SUB, COLS), F32)
        if it > 0:
            rows = jnp.where(sub_pos == MODES, numer, rows)
            rows = jnp.where(sub_pos == MODES + 1, denom, rows)
        ref[a, b] = rows
        gather_send(it + 1, ref, span)
        if it < ITERS:
            value = dot3(s.e_high[...], s.e_low[...], s.x_high[...], s.x_low[...])
            for k in range(2):
                for j in range(H):
                    line = (k * H + j) * ES
                    for h in range(HV):
                        s.zs_col[it, k, h, j] = value[line : line + ES, half(h)]
            for k in range(4):
                u0 = hi if k // 2 else lo
                skip = ((H - 1) * (k // 2), (H - 1) * (k % 2))
                n = 0
                for r in range(H):
                    for j in range(H):
                        if (r, j) == ((H - 1) - skip[0], (H - 1) - skip[1]):
                            continue
                        for h in range(HV):
                            s.zs_cor[it, k, h, n : n + 1, :] = s.zs_col[
                                it, k % 2, h, j, u0 + r : u0 + r + 1, :
                            ]
                        n += 1
            copies = exchange(
                4 + it,
                lambda i: s.zs_row.at[it, i],
                lambda i: s.zs_col.at[it, i],
                lambda i: s.zs_cor.at[it, i],
            )
            send(copies, SIDES)
            if it == 0:
                lax.fori_loop(0, LOCAL // step, left_side_perm, 0)

            def solve(i, carry):
                rows = pl.ds(pl.multiple_of(i * step, step), step)
                value = dot3(s.l_high[rows, :], s.l_low[rows, :], s.x_high[...], s.x_low[...])
                for j in range(step // ES):
                    u = i * (step // ES) + j
                    for h in range(HV):
                        s.wdeep[h, pl.ds(at(u, 0), ES), :] = value[j * ES : (j + 1) * ES, half(h)]
                return carry

            lax.fori_loop(0, LOCAL // step, solve, 0)
            for k, u in enumerate((lo, hi)):
                for h in range(HV):
                    for r in range(H):
                        s.zs_row[it, k, h, r] = s.wdeep[h, pl.ds(at(u + r, 0), ES), :]
            send(copies, ENDS)
            pending.append(copies)
        if it == 0:
            build_phi()
            build_kmat()
        if it >= 2:
            old = sizes[it - 2]

            def advance(i, carry):
                for h in range(HV):
                    here = s.deep[it % 2, h, pl.ds(at(OV + i, OV), CS), :]
                    s.sol[h, i, 0:CS, :] = s.sol[h, i, 0:CS, :] + old[:, half(h)] * here
                return carry

            lax.fori_loop(0, CS, advance, 0)
        gather_recv(it + 1, ref, span)
        everyone = ref[...].reshape(N * W, SUB, COLS)
        if it > 0:
            total = jnp.sum(everyone, axis=0)
            size = total[MODES : MODES + 1] / total[MODES + 1 : MODES + 2]
            sizes.append(size)
        if it == ITERS:
            break
        coarse_only = lax.broadcasted_iota(jnp.int32, everyone.shape, 1) < MODES
        everyone = jnp.where(coarse_only, everyone, 0.0)
        g_high, g_low = split(everyone.reshape(N * W * SUB, COLS))
        s_high, s_low = split(dot3(s.kmat[0], s.kmat[1], g_high, g_low))
        if 2 * LK <= LANES:
            s_all = jnp.concatenate([s_high, s_low], axis=0)
        else:
            s_all = jnp.concatenate([s_high, s_high, s_low], axis=0)
        recv(copies)
        for h in range(HV):
            for k in range(2):
                for j in range(H):
                    deep_line = k * (CS + H) + j
                    s.wdeep[h, pl.ds(deep_line * DW + H, CS), :] = s.z_row[
                        it, k, h, j, OV : OV + CS, :
                    ]
                    s.wdeep[h, pl.ds(H * DW + deep_line, CS, stride=DW), :] = s.z_col[
                        it, k, h, j, OV : OV + CS, :
                    ]
            for k in range(4):
                skip = ((H - 1) * (k // 2), (H - 1) * (k % 2))
                n = 0
                for r in range(H):
                    for j in range(H):
                        if (r, j) == skip:
                            continue
                        cell = ((k // 2) * (CS + H) + r) * DW + (k % 2) * (CS + H) + j
                        s.wdeep[h, pl.ds(cell, 1), :] = s.z_cor[it, k, h, n : n + 1, :]
                        n += 1
        chunk = RP // 2
        now, before = it % 2, 1 - it % 2

        def coarse_part(i, carry):
            rows = pl.ds(pl.multiple_of(i * chunk, chunk), chunk)
            value = dot(s.phi[rows, :], s_all)
            for h in range(HV):
                part = value[:, half(h)] + s.wdeep[h, rows, :]
                if it > 0:
                    part = s.deep[before, h, rows, :] - size[:, half(h)] * part
                s.deep[now, h, rows, :] = part
            return carry

        lax.fori_loop(0, 2, coarse_part, 0)
        read = lambda h, rows: s.deep[now, h, rows, :]
        if it < ITERS - 1:

            def margin(q, carry):
                u = jnp.where(q < OV, q, q + CS)
                set_x(u, operator(read, u, 0, ES))
                return carry

            lax.fori_loop(0, 2 * OV, margin, 0)

        def apply(i, carry):
            u = OV + i
            value = operator(read, u, 0, ES)
            if it < ITERS - 1:
                set_x(u, value)
            line = pl.ds(pl.multiple_of(u * ES, ES), ES)
            sums = []
            for h in range(HV):
                left = s.res[h, line, :]
                if it > 0:
                    left = left - size[:, half(h)] * s.img[h, i]
                    s.res[h, line, :] = left
                s.img[h, i] = value[h]
                sums.append(carry[2 * h] + left * value[h])
                sums.append(carry[2 * h + 1] + value[h] * value[h])
            return tuple(sums)

        nothing = jnp.zeros((ES, LANES), F32)
        sums = lax.fori_loop(0, CS, apply, (nothing,) * (2 * HV))
        col = lax.broadcasted_iota(jnp.int32, (ES, LANES), 0)
        mine = (col >= OV) & (col < OV + CS)
        sums = [jnp.sum(jnp.where(mine, v, 0.0), axis=0, keepdims=True) for v in sums]
        numer = jnp.concatenate(sums[0::2], axis=1)
        denom = jnp.concatenate(sums[1::2], axis=1)

    size = sizes[-1]

    def finish(i, carry):
        u = OV + i
        for h in range(HV):
            step_of = size[:, half(h)]
            here = s.deep[(ITERS - 1) % 2, h, pl.ds(at(u, OV), CS), :]
            sol_out[i, :, half(h)] = s.sol[h, i, 0:CS, :] + step_of * here
            here = s.img[h, i, OV : OV + CS, :]
            res_out[i, :, half(h)] = s.res[h, pl.ds(u * ES + OV, CS), :] - step_of * here
        return carry

    lax.fori_loop(0, CS, finish, 0)
    for copies in pending:
        done(copies)
    gather_done(0, s.k0, k_rows)
    for it in range(ITERS + 1):
        gather_done(it + 1, s.g.at[it], spans[it])


def local(
    N,
    W,
    right_side,
    initial_guess,
    class_map,
    class_conductivity,
    window_index,
    local_inverse,
    coarse_basis,
    coarse_inverse,
):
    CS, _, COLS = right_side.shape
    MODES, LOCAL = coarse_basis.shape[2:]
    ES = math.isqrt(LOCAL)
    OV = (ES - CS) // 2
    H = OV + 1
    DW = ES + 2
    RP = -(-DW * DW // 32) * 32
    HV = COLS // LANES
    KR = coarse_inverse.size // COLS
    K0 = -(-KR // SUB) * SUB
    CHIPS = N * W // 2
    PK = (2 if 6 * MODES * N <= LANES else 3) * LANES
    TALL = -(-DW // SUB) * SUB
    vmem = pl.BlockSpec(memory_space=pltpu.VMEM)
    scratch = dict(
        inv=((LOCAL, LOCAL), F32),
        perm=((LOCAL, LOCAL), BF16),
        perm_t=((LOCAL, LOCAL), BF16),
        t_high=((LOCAL, LOCAL), BF16),
        t_low=((LOCAL, LOCAL), BF16),
        l_high=((LOCAL, LOCAL), BF16),
        l_low=((LOCAL, LOCAL), BF16),
        e_high=((2 * H * ES, LOCAL), BF16),
        e_low=((2 * H * ES, LOCAL), BF16),
        bw=((2 * SUB, LOCAL), BF16),
        spread=((LANES, LOCAL), F32),
        x_high=((LOCAL, COLS), BF16),
        x_low=((LOCAL, COLS), BF16),
        field=((LANES, LANES), F32),
        cfield=((ES, LANES), F32),
        cst=((3, TALL, LANES), F32),
        cond=((RP, LANES), F32),
        wt=((5, LOCAL, LANES), F32),
        gd=((HV, RP, LANES), F32),
        sol=((HV, CS, ES, LANES), F32),
        res=((HV, LOCAL, LANES), F32),
        img=((HV, CS, ES, LANES), F32),
        aux=((LOCAL, LANES), F32),
        daux=((RP, LANES), F32),
        phi=((RP, PK), BF16),
        wdeep=((HV, RP, LANES), F32),
        deep=((2, HV, RP, LANES), F32),
        kmat=((2, LANES, N * W * SUB), BF16),
        k0=((N, W, K0, COLS), F32),
        g=((ITERS + 1, N, W, SUB, COLS), F32),
        gs_col=((2, CS, COLS), F32),
        g_row=((2, CS, COLS), F32),
        g_col=((2, CS, COLS), F32),
        c_row=((2, ES, LANES), F32),
        c_col=((2, SUB, LANES), F32),
        c_cor=((4, SUB, LANES), F32),
        as_col=((2, H, ES, LANES), F32),
        a_row=((2, H * ES, LANES), F32),
        a_col=((2, H, ES, LANES), F32),
        a_cor=((4, H, SUB, LANES), F32),
        rs_row=((2, HV, OV * ES, LANES), F32),
        rs_col=((2, HV, OV, ES, LANES), F32),
        rs_cor=((4, HV, SUB, LANES), F32),
        r_row=((2, HV, OV * ES, LANES), F32),
        r_col=((2, HV, OV, ES, LANES), F32),
        r_cor=((4, HV, SUB, LANES), F32),
        zs_row=((ITERS, 2, HV, H, ES, LANES), F32),
        zs_col=((ITERS, 2, HV, H, ES, LANES), F32),
        zs_cor=((ITERS, 4, HV, SUB, LANES), F32),
        z_row=((ITERS, 2, HV, H, ES, LANES), F32),
        z_col=((ITERS, 2, HV, H, ES, LANES), F32),
        z_cor=((ITERS, 4, HV, SUB, LANES), F32),
    )
    shapes = {name: pltpu.VMEM(*spec) for name, spec in scratch.items()}
    dma = pltpu.SemaphoreType.DMA
    shapes |= dict(
        ssem=dma((ITERS + 4, 8)),
        rsem=dma((ITERS + 4, 8)),
        gs=dma((ITERS + 2, CHIPS)),
        gr=dma((ITERS + 2, CHIPS)),
        fs=dma((ITERS + 2, CHIPS)),
        fr=dma((ITERS + 2, CHIPS)),
        lsem=dma,
    )
    anywhere = pl.BlockSpec(memory_space=pl.ANY)
    smem = pl.BlockSpec(memory_space=pltpu.SMEM)
    return pl.pallas_call(
        functools.partial(kernel, (N, W, ES, OV, CS, COLS, MODES, KR), tuple(shapes)),
        out_shape=(jax.ShapeDtypeStruct(right_side.shape, F32),) * 2,
        in_specs=[vmem] * 3 + [smem, vmem, anywhere] + [vmem] * 2,
        out_specs=(vmem, vmem),
        scratch_shapes=list(shapes.values()),
        compiler_params=pltpu.CompilerParams(
            collective_id=0, has_side_effects=True, vmem_limit_bytes=60 * 1024 * 1024
        ),
        name="schwarz",
    )(
        right_side,
        initial_guess,
        class_map,
        class_conductivity,
        window_index[0],
        local_inverse[0, 0],
        coarse_basis,
        coarse_inverse,
    )


def solution(mesh):
    in_specs = (
        P("narrow", "wide", None),
        P("narrow", "wide", None),
        P("narrow", "wide"),
        P(),
        P("narrow", "wide", None),
        P("narrow", "wide", None, None),
        P("narrow", "wide", None, None),
        P("wide", "narrow"),
    )
    out_specs = (P("narrow", "wide", None), P("narrow", "wide", None))
    body = functools.partial(local, mesh.shape["narrow"], mesh.shape["wide"])
    return jax.shard_map(body, mesh=mesh, in_specs=in_specs, out_specs=out_specs, check_vma=False)
```

time: 79.7 us -> 69.5 us (0.87)
  Pallas kernels: 78.8 us -> 64.2 us
  local copies, waits for them, and re-layouts: 0 us -> 4.4 us
    pallas_call x1, Pallas kernels: 74.7 us -> 64.2 us  [local(): pl.pallas_call(functools.partial(kernel, (N, W, ES, OV, CS, COLS, MODES,...]
    unnamed x0 -> x2, local copies, waits for them, and re-layouts: none -> 4.4 us
    pallas_call x1 -> x0, Pallas kernels: 4.15 us -> none  [local(): pl.pallas_call(functools.partial(finish, OV, CS), grid=(CS // block,), ou...]
where the time goes in v1:
time: 69.5 us; the launch traced here: 69.3 us
  Pallas kernels  64.2 us (92%)
  local copies, waits for them, and re-layouts  4.4 us (6%)
    pallas_call x1, Pallas kernels, local(): pl.pallas_call(functools.partial(kernel, (N, W, ES, OV, CS, COLS, MODES,...  64.2 us
    unnamed x2, local copies, waits for them, and re-layouts  4.4 us

profile of v1, /device:TPU:1, one launch (start us, length us, event | category | flops | bytes accessed | tf_op | source)
XLA Modules:
  0.0 69.3 jit_solution(9880976686352583031)
XLA Ops:
  0.6 64.2 %schwarz.1 = (f32[28,28,256]{2,1,0:T(8,128)}, f32[28,28,256]{2,1,0:T(8,128)}) custom-call(f32[28,28,256]{2,1,0:T(8,128)} %refs_0_.1, f32[28,28,256]{2,1,0:T(8,128)} %refs_1_.1, s32[28,28]{1,0:T(8,128)} %refs_2_.1, f32[8]{0:T(128)} %refs_3_.1, s32[1,1024]{1,0:T(1,128)} %bitcast.3, f32[1024,1024]{1,0:T(8,128)} %bitcast.2, f32[1,1,4,1024]{3,2,1,0:T(4,128)} %refs_6_.1, ...), custom_call_target="tpu_custom_call" | custom-call | tf_op jit(solution)/shard_map/schwarz/pallas_call | solution.py:785
  64.9 2.2 %copy.12 = f32[28,28,256]{2,1,0:T(8,128)} copy(f32[28,28,256]{2,1,0:T(8,128)} %get-tuple-element.4) | data formatting | bytes 1605632
  67.1 2.2 %copy.13 = f32[28,28,256]{2,1,0:T(8,128)} copy(f32[28,28,256]{2,1,0:T(8,128)} %get-tuple-element.5) | data formatting | bytes 1605632

commit v2 on v1

--- a/solution.py
+++ b/solution.py
@@ -121,6 +121,7 @@
 
     def exchange(slot, rows, cols, corners):
         copies = {}
+        lane = slot if slot < 4 else 4 + slot % 2
         for d in range(8):
             if corners is None and 0 not in DIRS[d]:
                 continue
@@ -130,8 +131,8 @@
             copies[d] = pltpu.make_async_remote_copy(
                 src_ref=landing(d, rows, cols, corners, False),
                 dst_ref=landing(d, pick(to[0]), pick(to[1]), to[2] is not None and pick(to[2]), True),
-                send_sem=s.ssem.at[slot, d],
-                recv_sem=s.rsem.at[slot, 7 - d],
+                send_sem=s.ssem.at[lane, d],
+                recv_sem=s.rsem.at[lane, 7 - d],
                 device_id=(b + db, a + da),
                 device_id_type=MESH,
             )
@@ -159,7 +160,11 @@
             def _():
                 copies[d].wait_send()
 
+    def place_of(slot):
+        return 2 if slot == 0 else (slot - 1) % 2
+
     def gather_copy(slot, k, ref, rows):
+        slot = place_of(slot)
         _, target = other(k)
         part = ref.at[a, b, rows]
         return pltpu.make_async_remote_copy(
@@ -172,6 +177,7 @@
         )
 
     def forward(slot, k, ref, rows, mine):
+        slot = place_of(slot)
         idx, _ = other(k)
         row = 2 * (idx // W)
         part = ref.at[row + core, lax.rem(idx, W), rows]
@@ -186,11 +192,16 @@
         )
 
     def gather_send(slot, ref, rows):
-        def body(k, carry):
-            gather_copy(slot, k, ref, rows).start()
-            return carry
-
-        lax.fori_loop(1, CHIPS, body, 0)
+        if CHIPS <= 16:
+            for k in range(1, CHIPS):
+                gather_copy(slot, k, ref, rows).start()
+        else:
+
+            def body(k, carry):
+                gather_copy(slot, k, ref, rows).start()
+                return carry
+
+            lax.fori_loop(1, CHIPS, body, 0)
         forward(slot, 0, ref, rows, True).start()
 
     def gather_recv(slot, ref, rows):
@@ -199,8 +210,8 @@
             pltpu.make_async_remote_copy(
                 src_ref=ref.at[a, b, rows],
                 dst_ref=ref.at[target[1], target[0], rows],
-                send_sem=s.gs.at[slot, k],
-                recv_sem=s.gr.at[slot, idx],
+                send_sem=s.gs.at[place_of(slot), k],
+                recv_sem=s.gr.at[place_of(slot), idx],
                 device_id=target,
                 device_id_type=MESH,
             ).wait_recv()
@@ -264,10 +275,17 @@
     for c in range(0, LOCAL, LANES):
         s.perm_t[:, c : c + LANES] = jnp.where(lane + c == tall_numbering, 1.0, 0.0).astype(BF16)
 
+    NE = 2 * H * ES
+    line = lax.broadcasted_iota(jnp.int32, (NE, LOCAL), 0)
+    col = line >> int(math.log2(ES))
+    col = jnp.where(col < H, col + lo, col - H + hi)
+    pos = (line & (ES - 1)) * ES + col
+    s.perm[0:NE, :] = jnp.where(pos == numbering, 1.0, 0.0).astype(BF16)
+
     def hot(i, carry):
         off = pl.multiple_of(i * step, step)
         pos = lax.broadcasted_iota(jnp.int32, (step, LOCAL), 0) + off
-        s.perm[pl.ds(off, step), :] = jnp.where(pos == numbering, 1.0, 0.0).astype(BF16)
+        s.perm[pl.ds(NE + off, step), :] = jnp.where(pos == numbering, 1.0, 0.0).astype(BF16)
         return carry
 
     lax.fori_loop(0, LOCAL // step, hot, 0)
@@ -278,7 +296,8 @@
     for m in range(MODES):
         s.spread[...] = jnp.where(line == m, basis[m : m + 1], s.spread[...])
     b_high, b_low = split(jnp.transpose(s.spread[...]))
-    s.aux[...] = dot(s.perm[...], b_high) + dot(s.perm[...], b_low)
+    both = dot(s.perm[NE:, :], jnp.concatenate([b_high, b_low], axis=1))
+    s.aux[...] = both[:, 0:LANES] + both[:, LANES:]
     for k, first in enumerate((lo, hi)):
         for j in range(H):
             s.as_col[k, j] = s.aux[pl.ds(first + j, ES, stride=ES), :]
@@ -384,18 +403,12 @@
     def right_side_perm(i, carry):
         rows = pl.ds(pl.multiple_of(i * step, step), step)
         high, low = split(s.inv[rows, :])
-        s.t_high[rows, :] = dot(high, s.perm_t[...]).astype(BF16)
-        s.t_low[rows, :] = dot(low, s.perm_t[...]).astype(BF16)
+        both = dot(jnp.concatenate([high, low], axis=0), s.perm_t[...]).astype(BF16)
+        s.t_high[rows, :] = both[0:step]
+        s.t_low[rows, :] = both[step:]
         return carry
 
     lax.fori_loop(0, LOCAL // step, right_side_perm, 0)
-    line = lax.broadcasted_iota(jnp.int32, (2 * H * ES, LOCAL), 0)
-    col = line >> int(math.log2(ES))
-    col = jnp.where(col < H, col + lo, col - H + hi)
-    pos = (line & (ES - 1)) * ES + col
-    edge = jnp.where(pos == numbering, 1.0, 0.0).astype(BF16)
-    s.e_high[...] = dot(edge, s.t_high[...]).astype(BF16)
-    s.e_low[...] = dot(edge, s.t_low[...]).astype(BF16)
     m_high, m_low = split(jnp.concatenate([basis, jnp.zeros((SUB - MODES, LOCAL), F32)], axis=0))
     s.bw[...] = dot(jnp.concatenate([m_high, m_low], axis=0), s.perm_t[...]).astype(BF16)
 
@@ -430,7 +443,8 @@
         return both[0:SUB] + (both[SUB:] + dot(s.bw[0:SUB, :], s.x_low[...]))
 
     def left_side_perm(i, carry):
-        rows = pl.ds(pl.multiple_of(i * step, step), step)
+        big = (NE + LOCAL) // 2
+        rows = pl.ds(pl.multiple_of(i * big, big), big)
         s.l_high[rows, :] = dot(s.perm[rows, :], s.t_high[...]).astype(BF16)
         s.l_low[rows, :] = dot(s.perm[rows, :], s.t_low[...]).astype(BF16)
         return carry
@@ -525,7 +539,9 @@
         ref[a, b] = rows
         gather_send(it + 1, ref, span)
         if it < ITERS:
-            value = dot3(s.e_high[...], s.e_low[...], s.x_high[...], s.x_low[...])
+            if it == 0:
+                left_side_perm(0, 0)
+            value = dot3(s.l_high[0:NE, :], s.l_low[0:NE, :], s.x_high[...], s.x_low[...])
             for k in range(2):
                 for j in range(H):
                     line = (k * H + j) * ES
@@ -552,10 +568,10 @@
             )
             send(copies, SIDES)
             if it == 0:
-                lax.fori_loop(0, LOCAL // step, left_side_perm, 0)
+                left_side_perm(1, 0)
 
             def solve(i, carry):
-                rows = pl.ds(pl.multiple_of(i * step, step), step)
+                rows = pl.ds(NE + pl.multiple_of(i * step, step), step)
                 value = dot3(s.l_high[rows, :], s.l_low[rows, :], s.x_high[...], s.x_low[...])
                 for j in range(step // ES):
                     u = i * (step // ES) + j
@@ -573,6 +589,12 @@
         if it == 0:
             build_phi()
             build_kmat()
+            for early in pending[0:4]:
+                done(early)
+            gather_done(0, s.k0, k_rows)
+        else:
+            done(pending[3 + it])
+            gather_done(it, s.g.at[it - 1], spans[it - 1])
         if it >= 2:
             old = sizes[it - 2]
 
@@ -682,11 +704,7 @@
         return carry
 
     lax.fori_loop(0, CS, finish, 0)
-    for copies in pending:
-        done(copies)
-    gather_done(0, s.k0, k_rows)
-    for it in range(ITERS + 1):
-        gather_done(it + 1, s.g.at[it], spans[it])
+    gather_done(ITERS + 1, s.g.at[ITERS], spans[ITERS])
 
 
 def local(
@@ -717,14 +735,12 @@
     vmem = pl.BlockSpec(memory_space=pltpu.VMEM)
     scratch = dict(
         inv=((LOCAL, LOCAL), F32),
-        perm=((LOCAL, LOCAL), BF16),
+        perm=((2 * H * ES + LOCAL, LOCAL), BF16),
         perm_t=((LOCAL, LOCAL), BF16),
         t_high=((LOCAL, LOCAL), BF16),
         t_low=((LOCAL, LOCAL), BF16),
-        l_high=((LOCAL, LOCAL), BF16),
-        l_low=((LOCAL, LOCAL), BF16),
-        e_high=((2 * H * ES, LOCAL), BF16),
-        e_low=((2 * H * ES, LOCAL), BF16),
+        l_high=((2 * H * ES + LOCAL, LOCAL), BF16),
+        l_low=((2 * H * ES + LOCAL, LOCAL), BF16),
         bw=((2 * SUB, LOCAL), BF16),
         spread=((LANES, LOCAL), F32),
         x_high=((LOCAL, COLS), BF16),
@@ -772,19 +788,19 @@
     shapes = {name: pltpu.VMEM(*spec) for name, spec in scratch.items()}
     dma = pltpu.SemaphoreType.DMA
     shapes |= dict(
-        ssem=dma((ITERS + 4, 8)),
-        rsem=dma((ITERS + 4, 8)),
-        gs=dma((ITERS + 2, CHIPS)),
-        gr=dma((ITERS + 2, CHIPS)),
-        fs=dma((ITERS + 2, CHIPS)),
-        fr=dma((ITERS + 2, CHIPS)),
+        ssem=dma((6, 8)),
+        rsem=dma((6, 8)),
+        gs=dma((3, CHIPS)),
+        gr=dma((3, CHIPS)),
+        fs=dma((3, CHIPS)),
+        fr=dma((3, CHIPS)),
         lsem=dma,
     )
     anywhere = pl.BlockSpec(memory_space=pl.ANY)
     smem = pl.BlockSpec(memory_space=pltpu.SMEM)
-    return pl.pallas_call(
+    fields = pl.pallas_call(
         functools.partial(kernel, (N, W, ES, OV, CS, COLS, MODES, KR), tuple(shapes)),
-        out_shape=(jax.ShapeDtypeStruct(right_side.shape, F32),) * 2,
+        out_shape=(pltpu.VMEM(right_side.shape, F32),) * 2,
         in_specs=[vmem] * 3 + [smem, vmem, anywhere] + [vmem] * 2,
         out_specs=(vmem, vmem),
         scratch_shapes=list(shapes.values()),
@@ -802,6 +818,7 @@
         coarse_basis,
         coarse_inverse,
     )
+    return tuple(fields)
 
 
 def solution(mesh):

time: 69.5 us -> 63.3 us (0.911)
  Pallas kernels: 64.2 us -> 60.7 us
  local copies, waits for them, and re-layouts: 4.4 us -> 1.85 us
    pallas_call x1, Pallas kernels: 64.2 us -> 60.7 us  [local(): pl.pallas_call(functools.partial(kernel, (N, W, ES, OV, CS, COLS, MODES,...]
    unnamed x2, local copies, waits for them, and re-layouts: 4.4 us -> 1.85 us
where the time goes in v2:
time: 63.3 us; the launch traced here: 63.2 us
  Pallas kernels  60.7 us (96%)
  local copies, waits for them, and re-layouts  1.85 us (3%)
  between operations  0.64 us (1%)
    pallas_call x1, Pallas kernels, local(): pl.pallas_call(functools.partial(kernel, (N, W, ES, OV, CS, COLS, MODES,...  60.7 us
    unnamed x2, local copies, waits for them, and re-layouts  1.85 us

profile of v2, /device:TPU:1, one launch (start us, length us, event | category | flops | bytes accessed | tf_op | source)
XLA Modules:
  0.0 63.2 jit_solution(2360018268380165265)
XLA Ops:
  0.6 60.7 %schwarz.1 = (f32[28,28,256]{2,1,0:T(8,128)S(1)}, f32[28,28,256]{2,1,0:T(8,128)S(1)}) custom-call(f32[28,28,256]{2,1,0:T(8,128)} %refs_0_.1, f32[28,28,256]{2,1,0:T(8,128)} %refs_1_.1, s32[28,28]{1,0:T(8,128)} %refs_2_.1, f32[8]{0:T(128)} %refs_3_.1, s32[1,1024]{1,0:T(1,128)} %bitcast.3, f32[1024,1024]{1,0:T(8,128)} %bitcast.2, f32[1,1,4,1024]{3,2,1,0:T(4,128)} %refs_6_.1, ...), custom_call_target="tpu_custom_call" | custom-call | tf_op jit(solution)/shard_map/schwarz/pallas_call | solution.py:801
  61.3 0.9 %copy.12 = f32[28,28,256]{2,1,0:T(8,128)} copy(f32[28,28,256]{2,1,0:T(8,128)S(1)} %get-tuple-element.2) | data formatting | bytes 1605632
  62.3 0.9 %copy.13 = f32[28,28,256]{2,1,0:T(8,128)} copy(f32[28,28,256]{2,1,0:T(8,128)S(1)} %get-tuple-element.3) | data formatting | bytes 1605632

commit v3 on v2

--- a/solution.py
+++ b/solution.py
@@ -191,17 +191,19 @@
             device_id_type=MESH,
         )
 
+    def each(first, body):
+        if CHIPS <= 16:
+            for k in range(first, CHIPS):
+                body(k, 0)
+        else:
+            lax.fori_loop(first, CHIPS, body, 0)
+
     def gather_send(slot, ref, rows):
-        if CHIPS <= 16:
-            for k in range(1, CHIPS):
-                gather_copy(slot, k, ref, rows).start()
-        else:
-
-            def body(k, carry):
-                gather_copy(slot, k, ref, rows).start()
-                return carry
-
-            lax.fori_loop(1, CHIPS, body, 0)
+        def body(k, carry):
+            gather_copy(slot, k, ref, rows).start()
+            return carry
+
+        each(1, body)
         forward(slot, 0, ref, rows, True).start()
 
     def gather_recv(slot, ref, rows):
@@ -218,13 +220,13 @@
             forward(slot, k, ref, rows, True).start()
             return carry
 
-        lax.fori_loop(1, CHIPS, relay, 0)
+        each(1, relay)
 
         def collect(k, carry):
             forward(slot, k, ref, rows, False).wait_recv()
             return carry
 
-        lax.fori_loop(0, CHIPS, collect, 0)
+        each(0, collect)
 
     def gather_done(slot, ref, rows):
         def body(k, carry):
@@ -401,14 +403,15 @@
     load.wait()
 
     def right_side_perm(i, carry):
-        rows = pl.ds(pl.multiple_of(i * step, step), step)
+        tall = 2 * step
+        rows = pl.ds(pl.multiple_of(i * tall, tall), tall)
         high, low = split(s.inv[rows, :])
         both = dot(jnp.concatenate([high, low], axis=0), s.perm_t[...]).astype(BF16)
-        s.t_high[rows, :] = both[0:step]
-        s.t_low[rows, :] = both[step:]
-        return carry
-
-    lax.fori_loop(0, LOCAL // step, right_side_perm, 0)
+        s.t_high[rows, :] = both[0:tall]
+        s.t_low[rows, :] = both[tall:]
+        return carry
+
+    lax.fori_loop(0, LOCAL // (2 * step), right_side_perm, 0)
     m_high, m_low = split(jnp.concatenate([basis, jnp.zeros((SUB - MODES, LOCAL), F32)], axis=0))
     s.bw[...] = dot(jnp.concatenate([m_high, m_low], axis=0), s.perm_t[...]).astype(BF16)
 
@@ -541,7 +544,9 @@
         if it < ITERS:
             if it == 0:
                 left_side_perm(0, 0)
-            value = dot3(s.l_high[0:NE, :], s.l_low[0:NE, :], s.x_high[...], s.x_low[...])
+            high = s.l_high[0:NE, :]
+            both = dot(jnp.concatenate([high, s.l_low[0:NE, :]], axis=0), s.x_high[...])
+            value = both[0:NE] + (both[NE:] + dot(high, s.x_low[...]))
             for k in range(2):
                 for j in range(H):
                     line = (k * H + j) * ES
@@ -572,7 +577,9 @@
 
             def solve(i, carry):
                 rows = pl.ds(NE + pl.multiple_of(i * step, step), step)
-                value = dot3(s.l_high[rows, :], s.l_low[rows, :], s.x_high[...], s.x_low[...])
+                high = s.l_high[rows, :]
+                both = dot(jnp.concatenate([high, s.l_low[rows, :]], axis=0), s.x_high[...])
+                value = both[0:step] + (both[step:] + dot(high, s.x_low[...]))
                 for j in range(step // ES):
                     u = i * (step // ES) + j
                     for h in range(HV):

time: 63.3 us -> 62.6 us (0.989)
  Pallas kernels: 60.7 us -> 60 us
    pallas_call x1, Pallas kernels: 60.7 us -> 60 us  [local(): pl.pallas_call(functools.partial(kernel, (N, W, ES, OV, CS, COLS, MODES,...]
where the time goes in v3:
time: 62.6 us; the launch traced here: 62.5 us
  Pallas kernels  60 us (96%)
  local copies, waits for them, and re-layouts  1.85 us (3%)
  between operations  0.64 us (1%)
    pallas_call x1, Pallas kernels, local(): pl.pallas_call(functools.partial(kernel, (N, W, ES, OV, CS, COLS, MODES,...  60 us
    unnamed x2, local copies, waits for them, and re-layouts  1.85 us

profile of v3, /device:TPU:1, one launch (start us, length us, event | category | flops | bytes accessed | tf_op | source)
XLA Modules:
  0.0 62.5 jit_solution(12767938201936394190)
XLA Ops:
  0.6 60.0 %schwarz.1 = (f32[28,28,256]{2,1,0:T(8,128)S(1)}, f32[28,28,256]{2,1,0:T(8,128)S(1)}) custom-call(f32[28,28,256]{2,1,0:T(8,128)} %refs_0_.1, f32[28,28,256]{2,1,0:T(8,128)} %refs_1_.1, s32[28,28]{1,0:T(8,128)} %refs_2_.1, f32[8]{0:T(128)} %refs_3_.1, s32[1,1024]{1,0:T(1,128)} %bitcast.3, f32[1024,1024]{1,0:T(8,128)} %bitcast.2, f32[1,1,4,1024]{3,2,1,0:T(4,128)} %refs_6_.1, ...), custom_call_target="tpu_custom_call" | custom-call | tf_op jit(solution)/shard_map/schwarz/pallas_call | solution.py:808
  60.6 0.9 %copy.12 = f32[28,28,256]{2,1,0:T(8,128)} copy(f32[28,28,256]{2,1,0:T(8,128)S(1)} %get-tuple-element.2) | data formatting | bytes 1605632
  61.6 0.9 %copy.13 = f32[28,28,256]{2,1,0:T(8,128)} copy(f32[28,28,256]{2,1,0:T(8,128)S(1)} %get-tuple-element.3) | data formatting | bytes 1605632
